TPU v7x, 256 devices: a whole 4x4x8 slice. The times are simulated.
256 devices in a mesh: band: 32 (over x_hi, z, core), var: 8 (over y, x_lo).
Axes of the slice: x: 4 (x_hi: 2, x_lo: 2; x = x_hi * 2 + x_lo), y: 4, z: 8, core: 2. Of those that a mesh axis runs over, the one named last changes fastest.
Arguments:
- patches: bfloat16 [16, 32, 256, 64], P('var', 'band'), may hold values from -6 to 6
- w_embed: bfloat16 [16, 64, 2048], P('var'), may hold values from -0.75 to 0.75
- var_bias: float32 [16, 2048], P('var'), may hold values from -3 to 3
- agg_gain: float32 [2048], replicated, may hold values from 0.1 to 1.9
- wq: bfloat16 [2048, 2048], P(None, 'var'), may hold values from -4 to 4
- wk: bfloat16 [2048, 2048], P(None, 'var'), may hold values from -4 to 4
- wv: bfloat16 [2048, 2048], P(None, 'var'), may hold values from -0.125 to 0.125
- wo: bfloat16 [2048, 2048], P('var'), may hold values from -0.125 to 0.125
- w_up: bfloat16 [2048, 1024], replicated, may hold values from -0.125 to 0.125
- conv1: bfloat16 [9, 64, 64], replicated, may hold values from -0.25 to 0.25
- bias1: float32 [64], replicated, may hold values from -3 to 3
- conv2: bfloat16 [9, 64, 64], replicated, may hold values from -0.25 to 0.25
- cotangent: bfloat16 [128, 64, 1024], P('band', None, 'var'), may hold values from -6 to 6
Outputs:
- field_out: bfloat16 [128, 64, 1024], P('band', None, 'var')
- grad_fine: bfloat16 [128, 64, 1024], P('band', None, 'var')
- grad_conv1: float32 [9, 64, 64], replicated
- grad_conv2: float32 [9, 64, 64], replicated
- grad_bias: float32 [64], replicated
All inputs are finite; a program needn't handle non-finite values.
Results may differ from a plain program's by a relative error of at most 0.03.
Values may be sent and summed in bfloat16 or wider, within the bound.
No kernel may reach another device: no remote copies, remote signals or barrier semaphores. Data moves between devices by JAX's collectives and lax.ppermute only.
A program may use at most 128 MiB of HBM per device.

v0:
```python
import math
import jax
import jax.numpy as jnp
from jax import lax
from jax.sharding import PartitionSpec as P

D = 2048
HD = 128
C = 64
R = 4


def with_halo(cells, sides, width):
    for axis, dim in sides:
        count = lax.axis_size(axis)
        ends = count - 1
        head = lax.slice_in_dim(cells, 0, width, axis=dim)
        tail = lax.slice_in_dim(cells, cells.shape[dim] - width, cells.shape[dim], axis=dim)
        cells = jnp.concatenate(
            [
                lax.ppermute(tail, axis, [(i, (i + 1) % count) for i in range(ends)]),
                cells,
                lax.ppermute(head, axis, [((i + 1) % count, i) for i in range(ends)]),
            ],
            axis=dim,
        )
    return cells


def tap_stack(padded, height, width):
    pieces = [
        padded[row_tap : row_tap + height, :, col_tap : col_tap + width]
        for row_tap in range(3)
        for col_tap in range(3)
    ]
    return jnp.concatenate(pieces, axis=1)


def conv_padded(padded, weight, height, width):
    stacked = tap_stack(padded, height, width)
    return jnp.einsum(
        "ykx,ko->yox",
        stacked,
        weight.reshape(-1, weight.shape[2]),
        preferred_element_type=jnp.float32,
    )


def flipped(weight):
    return jnp.transpose(weight[::-1], (0, 2, 1))


def weight_grad(padded, grads):
    stacked = tap_stack(padded, grads.shape[0], grads.shape[2])
    summed = jnp.einsum("ykx,yox->ko", stacked, grads, preferred_element_type=jnp.float32)
    return summed.reshape(9, padded.shape[1], grads.shape[1])


def normalize(mixed, agg_gain):
    return (
        mixed * lax.rsqrt(jnp.mean(mixed * mixed, axis=-1, keepdims=True) + 1e-05) * agg_gain
    ).astype(jnp.bfloat16)


def gradient_rim(field):
    return with_halo(field, (("band", 0), ("var", 2)), 1)


def on_device(
    patches, w_embed, var_bias, agg_gain, wq, wk, wv, wo, w_up, conv1, bias1, conv2, cotangent
):
    var_count = lax.axis_size("var")
    band_count = lax.axis_size("band")
    var_local, lat_dev, lon_all, patch_len = patches.shape
    lon_dev = lon_all // var_count
    flattened = jnp.transpose(patches, (1, 2, 0, 3)).reshape(
        lat_dev * lon_all, var_local * patch_len
    )
    partial_mix = jnp.dot(
        flattened, w_embed.reshape(var_local * patch_len, D), preferred_element_type=jnp.float32
    )
    partial_mix = (partial_mix + jnp.sum(var_bias, axis=0)).reshape(lat_dev, lon_all, D)
    mixed = lax.psum(partial_mix.astype(jnp.bfloat16), "var").astype(jnp.float32)
    normed_band = normalize(mixed, agg_gain)
    normed_slab = lax.dynamic_slice_in_dim(normed_band, lax.axis_index("var") * lon_dev, lon_dev, 1)
    token_rows = jnp.transpose(
        normed_band.reshape(lat_dev, var_count, lon_dev, D), (1, 0, 2, 3)
    ).reshape(-1, D)
    heads_local = wq.shape[1] // HD
    query_rows = token_rows.shape[0]
    queries = jnp.dot(token_rows, wq, preferred_element_type=jnp.float32).astype(jnp.bfloat16)
    keys_local = jnp.dot(token_rows, wk, preferred_element_type=jnp.float32).astype(jnp.bfloat16)
    values_local = jnp.dot(token_rows, wv, preferred_element_type=jnp.float32).astype(jnp.bfloat16)
    query_heads = queries.reshape(query_rows, heads_local, HD)
    running_max = jnp.full((heads_local, query_rows), -1e30, jnp.float32)
    key_heads = lax.all_gather(keys_local, "band", axis=0, tiled=True).reshape(-1, heads_local, HD)
    value_heads = lax.all_gather(values_local, "band", axis=0, tiled=True).reshape(
        -1, heads_local, HD
    )
    scores = jnp.einsum(
        "qhd,khd->hqk", query_heads, key_heads, preferred_element_type=jnp.float32
    ) / math.sqrt(HD)
    new_max = jnp.maximum(running_max, jnp.max(scores, axis=2))
    weights = jnp.exp(scores - new_max[:, :, None])
    new_sum = jnp.sum(weights, axis=2)
    update = jnp.einsum(
        "hqk,khd->hqd",
        weights.astype(jnp.bfloat16),
        value_heads,
        preferred_element_type=jnp.float32,
    )
    context = (update / new_sum[:, :, None]).astype(jnp.bfloat16)
    context = jnp.transpose(context, (1, 0, 2)).reshape(query_rows, heads_local * HD)
    slab_rows = lat_dev * lon_dev
    attended = lax.psum_scatter(
        jnp.dot(context, wo, preferred_element_type=jnp.float32).astype(jnp.bfloat16),
        "var",
        scatter_dimension=0,
        tiled=True,
    ).astype(jnp.float32)
    hidden = (normed_slab.reshape(slab_rows, D).astype(jnp.float32) + attended).astype(jnp.bfloat16)
    upsampled = jnp.dot(hidden, w_up, preferred_element_type=jnp.float32).astype(jnp.bfloat16)
    height = lat_dev * R
    width = lon_dev * R
    upsampled = jnp.transpose(
        upsampled.reshape(lat_dev, lon_dev, R, R, C), (0, 2, 4, 1, 3)
    ).reshape(height, C, width)
    bias_cols = bias1[None, :, None]
    fine_pad = with_halo(upsampled, (("band", 0), ("var", 2)), 1)
    pre = conv_padded(fine_pad, conv1, height, width) + bias_cols
    active = jax.nn.gelu(pre).astype(jnp.bfloat16)
    active_pad = with_halo(active, (("band", 0), ("var", 2)), 1)
    field_out = (
        conv_padded(active_pad, conv2, height, width) + upsampled.astype(jnp.float32)
    ).astype(jnp.bfloat16)
    cotangent_pad = gradient_rim(cotangent)
    d_active = conv_padded(cotangent_pad, flipped(conv2), height, width)
    d_pre = jax.vjp(jax.nn.gelu, pre)[1](d_active)[0].astype(jnp.bfloat16)
    d_pre_pad = gradient_rim(d_pre)
    grad_fine = (
        cotangent.astype(jnp.float32) + conv_padded(d_pre_pad, flipped(conv1), height, width)
    ).astype(jnp.bfloat16)
    factor = 1.0 / math.sqrt(height * band_count * width * var_count)
    first_terms = weight_grad(fine_pad, d_pre) * factor
    second_terms = weight_grad(active_pad, cotangent) * factor
    bias_terms = jnp.sum(d_pre.astype(jnp.float32), axis=(0, 2)) * factor
    grad_conv1, grad_conv2, grad_bias = lax.psum(
        (first_terms, second_terms, bias_terms), ("band", "var")
    )
    return (field_out, grad_fine, grad_conv1, grad_conv2, grad_bias)


def solution(mesh):
    in_specs = (
        P("var", "band", None, None),
        P("var", None, None),
        P("var", None),
        P(),
        P(None, "var"),
        P(None, "var"),
        P(None, "var"),
        P("var", None),
        P(),
        P(),
        P(),
        P(),
        P("band", None, "var"),
    )
    out_specs = (P("band", None, "var"), P("band", None, "var"), P(), P(), P())
    return jax.shard_map(
        on_device, mesh=mesh, in_specs=in_specs, out_specs=out_specs, check_vma=False
    )
```

profile of v0, /device:TPU:1, one launch (start us, length us, event | category | flops | bytes accessed | tf_op | source)
XLA Modules:
  0.0 733.0 jit_solution(12546269796696864949)
XLA Ops:
  8.1 2.5 fusion.10
  10.7 85.5 %all-reduce.4.cloned.1.call-done = bf16[1,256,2048]{2,1,0:T(8,128)(2,1)} async-done(((bf16[1,256,2048]{2,1,0:T(8,128)(2,1)}), bf16[1,256,2048]{2,1,0:T(8,128)(2,1)}) %all-reduce.4.cloned.1.call-update) | async-done | bytes 1048592 | tf_op jit(solution)/shard_map/psum | solution.py:83
  100.4 2.3 convolution_convert_fusion.1
  104.6 86.7 %all-gather.3.cloned.1.call-done = bf16[8192,256]{1,0:T(8,128)(2,1)} async-done(((bf16[256,256]{1,0:T(8,128)(2,1)}), bf16[8192,256]{1,0:T(8,128)(2,1)}) %all-gather.3.cloned.1.call-update) | async-done | bytes 4194320 | tf_op jit(solution)/shard_map/all_gather | solution.py:96
  191.3 9.3 %multiply_reduce_fusion = (f32[2,256]{1,0:T(2,128)S(1)}, f32[2,256,8192]{2,1,0:T(8,128)}) fusion(bf16[256,2,128]{0,2,1:T(8,128)(2,1)S(1)} %bitcast.117, bf16[8192,256]{1,0:T(8,128)(2,1)} %all-gather.3.cloned.1.call-done), kind=kOutput, calls=%fused_computation.1 | convolution fusion | flops 1082129920 | bytes 21104640 | tf_op jit(solution)/shard_map/qhd,khd->hqk/dot_general | solution.py:100
  200.6 8.8 %fusion = f32[2,256]{1,0:T(2,128)S(1)} fusion(f32[2,256,8192]{2,1,0:T(8,128)} %get-tuple-element.32, f32[2,256]{1,0:T(2,128)S(1)} %broadcast_maximum_fusion), kind=kLoop, calls=%fused_computation.2 | loop fusion | flops 12582400 | bytes 16781312 | tf_op jit(solution)/shard_map/reduce_sum | solution.py:105
  209.4 68.6 %all-gather.5.cloned.1.call-done = bf16[8192,256]{1,0:T(8,128)(2,1)} async-done(((bf16[256,256]{1,0:T(8,128)(2,1)}), bf16[8192,256]{1,0:T(8,128)(2,1)}) %all-gather.5.cloned.1.call-update) | async-done | bytes 4194320 | tf_op jit(solution)/shard_map/all_gather | solution.py:97
  278.0 6.4 copy.52
  284.4 10.4 %fusion.27 = bf16[256,2,128]{0,2,1:T(8,128)(2,1)S(1)} fusion(bf16[8192,2,128]{0,2,1:T(8,128)(2,1)} %bitcast.110, f32[2,256,8192]{2,1,0:T(8,128)} %get-tuple-element.32, f32[2,256]{1,0:T(2,128)S(1)} %broadcast_maximum_fusion, f32[256,2]{0,1:T(2,128)S(1)} %bitcast.125), kind=kOutput, calls=%fused_computation.38 | convolution fusion | flops 1086455808 | bytes 21106688 | tf_op jit(solution)/shard_map/hqk,khd->hqd/dot_general | solution.py:106
  296.4 3.0 collective-permute-start.8
  301.5 3.0 collective-permute-done.9
  304.6 2.2 collective-permute-start.10
  311.0 6.8 collective-permute-done.11
  321.3 11.4 %reduce-scatter.2.cloned.1.call-done = bf16[32,2048]{1,0:T(8,128)(2,1)} async-done(((bf16[256,2048]{1,0:T(8,128)(2,1)}), bf16[32,2048]{1,0:T(8,128)(2,1)}) %reduce-scatter.2.cloned.1.call-update) | async-done | bytes 131088 | tf_op jit(solution)/shard_map/reduce_scatter | solution.py:115
  332.7 3.1 convolution_convert_fusion.4
  336.1 8.2 %collective-permute-start = (bf16[1,64,128]{2,1,0:T(8,128)(2,1)S(1)}, bf16[1,64,128]{2,1,0:T(8,128)(2,1)S(1)}, u32[]{:S(2)}, u32[]{:S(2)}) collective-permute-start(bf16[1,64,128]{2,1,0:T(8,128)(2,1)S(1)} %copy.32), channel_id=1, source_target_pairs={{0,8},{8,16},{16,24},{24,32},{32,40},{40,48},{48,56},{56,64},{64,7... | collective-permute-start | bytes 49160 | tf_op jit(solution)/shard_map/ppermute | solution.py:21
  347.1 2.4 collective-permute-done.1
  353.2 3.3 collective-permute-done.3
  360.2 3.7 collective-permute-start.4
  365.8 3.6 collective-permute-start.12
  371.4 84.9 %psum.31 = f32[64]{0:T(128)} all-reduce(f32[64]{0:T(128)S(1)} %broadcast_multiply_fusion), channel_id=1, replica_groups=mesh['band'=32,'var'=8] {'band','var'}, use_global_device_ids=true, to_apply=%region_9.0 | all-reduce | flops 64 | bytes 512 | tf_op jit(solution)/shard_map/psum | solution.py:147
  459.1 4.0 collective-permute-start.14
  466.2 4.2 collective-permute-done.15
  472.8 250.3 %all-reduce.6.cloned.1.call-done = (f32[9,64,64]{2,1,0:T(8,128)}, f32[9,64,64]{2,1,0:T(8,128)}) async-done(((f32[9,64,64]{2,1,0:T(8,128)}, f32[9,64,64]{2,1,0:T(8,128)}), (f32[9,64,64]{2,1,0:T(8,128)}, f32[9,64,64]{2,1,0:T(8,128)})) %all-reduce.6.cloned.1.call-update) | async-done | bytes 294928 | tf_op jit(solution)/shard_map/psum | solution.py:147
  (126 shorter events, 44.0 us)
Async XLA Ops:
  7.2 287.6 %copy-start = (bf16[256,2048]{1,0:T(8,128)(2,1)S(1)}, bf16[256,2048]{1,0:T(8,128)(2,1)}, u32[]{:S(2)}) copy-start(bf16[256,2048]{1,0:T(8,128)(2,1)} %param.20) | copy-start | bytes 3145732
  7.2 92.1 %copy-start.2 = (bf16[2048,256]{1,0:T(8,128)(2,1)S(1)}, bf16[2048,256]{1,0:T(8,128)(2,1)}, u32[]{:S(2)}) copy-start(bf16[2048,256]{1,0:T(8,128)(2,1)} %param.18) | copy-start | bytes 3145732
  7.2 89.0 %all-reduce.4.cloned.1.call-start = ((), (), s32[]{:S(2)}) async-start(), calls=%async_computation.1 | async-start | bytes 2097152 | tf_op jit(solution)/shard_map/psum | solution.py:83
  10.6 180.7 %all-gather.3.cloned.1.call-start = ((), (), s32[]{:S(2)}) async-start(), calls=%async_computation.2 | async-start | bytes 4325376 | tf_op jit(solution)/shard_map/all_gather | solution.py:96
  100.4 177.6 %all-gather.5.cloned.1.call-start = ((), (), s32[]{:S(2)}) async-start(), calls=%async_computation.3 | async-start | bytes 4325376 | tf_op jit(solution)/shard_map/all_gather | solution.py:97
  102.8 229.9 %reduce-scatter.2.cloned.1.call-start = ((), (), s32[]{:S(2)}) async-start(), calls=%async_computation.4 | async-start | bytes 1179648 | tf_op jit(solution)/shard_map/reduce_scatter | solution.py:115
  296.3 426.7 %all-reduce.6.cloned.1.call-start = ((), (), s32[]{:S(2)}) async-start(), calls=%async_computation.5 | async-start | bytes 1179648 | tf_op jit(solution)/shard_map/psum | solution.py:147
  296.4 5.0 collective-permute-start.8
  299.4 5.1 collective-permute-start.9
  304.6 4.3 collective-permute-start.10
  307.1 10.6 %collective-permute-start.11 = (bf16[6,64,1]{2,1,0:T(8,128)(2,1)S(1)}, bf16[6,64,1]{2,1,0:T(8,128)(2,1)S(1)}, u32[]{:S(2)}, u32[]{:S(2)}) collective-permute-start(bf16[6,64,1]{2,1,0:T(8,128)(2,1)S(1)} %get-tuple-element.15), channel_id=1, source_target_pairs={{1,0},{2,1},{3,2},{4,3},{5,4},{6,5},{7,6},{9,8},{10,9},{11,10},{12... | collective-permute-start | bytes 2312 | tf_op jit(solution)/shard_map/ppermute | solution.py:23
  321.3 35.8 %copy-start.6 = (f32[64]{0:T(128)S(1)}, f32[64]{0:T(128)}, u32[]{:S(2)}) copy-start(f32[64]{0:T(128)} %param.23) | copy-start | bytes 772
  336.1 11.0 %collective-permute-start = (bf16[1,64,128]{2,1,0:T(8,128)(2,1)S(1)}, bf16[1,64,128]{2,1,0:T(8,128)(2,1)S(1)}, u32[]{:S(2)}, u32[]{:S(2)}) collective-permute-start(bf16[1,64,128]{2,1,0:T(8,128)(2,1)S(1)} %copy.32), channel_id=1, source_target_pairs={{0,8},{8,16},{16,24},{24,32},{32,40},{40,48},{48,56},{56,64},{64,7... | collective-permute-start | bytes 49160 | tf_op jit(solution)/shard_map/ppermute | solution.py:21
  344.4 5.1 collective-permute-start.1
  349.6 3.6 collective-permute-start.2
  351.2 5.4 collective-permute-start.3
  360.2 96.1 %collective-permute-start.4 = (bf16[1,64,128]{2,1,0:T(8,128)(2,1)S(1)}, bf16[1,64,128]{2,1,0:T(8,128)(2,1)S(1)}, u32[]{:S(2)}, u32[]{:S(2)}) collective-permute-start(bf16[1,64,128]{2,1,0:T(8,128)(2,1)S(1)} %get-tuple-element.29), channel_id=1, source_target_pairs={{0,8},{8,16},{16,24},{24,32},{32,40},{40,48},{48,56},{56,64},{64,7... | collective-permute-start | bytes 49160 | tf_op jit(solution)/shard_map/ppermute | solution.py:21
  363.8 92.4 %collective-permute-start.5 = (bf16[1,64,128]{2,1,0:T(8,128)(2,1)S(1)}, bf16[1,64,128]{2,1,0:T(8,128)(2,1)S(1)}, u32[]{:S(2)}, u32[]{:S(2)}) collective-permute-start(bf16[1,64,128]{2,1,0:T(8,128)(2,1)S(1)} %get-tuple-element.30), channel_id=1, source_target_pairs={{8,0},{16,8},{24,16},{32,24},{40,32},{48,40},{56,48},{64,56},{72,6... | collective-permute-start | bytes 49160 | tf_op jit(solution)/shard_map/ppermute | solution.py:23
  365.8 93.2 %collective-permute-start.12 = (bf16[1,64,128]{2,1,0:T(8,128)(2,1)S(1)}, bf16[1,64,128]{2,1,0:T(8,128)(2,1)S(1)}, u32[]{:S(2)}, u32[]{:S(2)}) collective-permute-start(bf16[1,64,128]{2,1,0:T(8,128)(2,1)S(1)} %get-tuple-element.25), channel_id=1, source_target_pairs={{0,8},{8,16},{16,24},{24,32},{32,40},{40,48},{48,56},{56,64},{64,7... | collective-permute-start | bytes 49160 | tf_op jit(solution)/shard_map/ppermute | solution.py:21
  369.4 89.6 %collective-permute-start.13 = (bf16[1,64,128]{2,1,0:T(8,128)(2,1)S(1)}, bf16[1,64,128]{2,1,0:T(8,128)(2,1)S(1)}, u32[]{:S(2)}, u32[]{:S(2)}) collective-permute-start(bf16[1,64,128]{2,1,0:T(8,128)(2,1)S(1)} %get-tuple-element.26), channel_id=1, source_target_pairs={{8,0},{16,8},{24,16},{32,24},{40,32},{48,40},{56,48},{64,56},{72,6... | collective-permute-start | bytes 49160 | tf_op jit(solution)/shard_map/ppermute | solution.py:23
  456.4 8.1 %collective-permute-start.6 = (bf16[6,64,1]{2,1,0:T(8,128)(2,1)S(1)}, bf16[6,64,1]{2,1,0:T(8,128)(2,1)S(1)}, u32[]{:S(2)}, u32[]{:S(2)}) collective-permute-start(bf16[6,64,1]{2,1,0:T(8,128)(2,1)S(1)} %get-tuple-element.20), channel_id=1, source_target_pairs={{0,1},{1,2},{2,3},{3,4},{4,5},{5,6},{6,7},{8,9},{9,10},{10,11},{11... | collective-permute-start | bytes 2312 | tf_op jit(solution)/shard_map/ppermute | solution.py:21
  457.7 6.8 collective-permute-start.7
  459.1 7.1 collective-permute-start.14
  463.1 7.3 collective-permute-start.15
  (4 other events, 49.1 us)
Sparse Core Ops, SparseCore 0:
  10.8 85.3 all-reduce.3
  100.5 90.7 all-gather.2
  194.7 83.2 all-gather.4
  296.4 36.2 reduce-scatter.1
  472.0 250.9 all-reduce.5
where the time goes:
time: 734 us; the launch traced here: 733 us
  waiting for transfers between devices  523 us (71%)
  blocking collectives  84.9 us (12%)
  starting transfers between devices  40.9 us (6%)
  matrix products  36.1 us (5%)
  other arithmetic  19.6 us (3%)
  local copies, waits for them, and re-layouts  14.5 us (2%)
  between operations  14.4 us (2%)
    psum x1, waiting for transfers between devices, on_device(): lax.psum((first_terms, second_terms, bias_terms), ('band', 'var'))  250 us
    all_gather x1, waiting for transfers between devices, on_device(): lax.all_gather(keys_local, 'band', axis=0, tiled=True)  86.7 us
    psum x1, waiting for transfers between devices, on_device(): lax.psum(partial_mix.astype(jnp.bfloat16), 'var').astype(jnp.float32)  85.5 us
    psum x1, blocking collectives, on_device(): lax.psum((first_terms, second_terms, bias_terms), ('band', 'var'))  84.9 us
    all_gather x1, waiting for transfers between devices, on_device(): lax.all_gather(values_local, 'band', axis=0, tiled=True)  68.6 us
    ppermute x8, starting transfers between devices, with_halo(): lax.ppermute(tail, axis, [(i, (i + 1) % count) for i in range(ends)])  27.6 us
    ppermute x8, waiting for transfers between devices, with_halo(): lax.ppermute(head, axis, [((i + 1) % count, i) for i in range(ends)])  19.7 us
  transfers between devices with their start and end apart: 21, of which 11 were waited for; matrix products, arithmetic and copies ran while one was open for 4% of the time, Pallas kernels for 0%

commit v1 on v0

--- a/solution.py
+++ b/solution.py
@@ -93,7 +93,9 @@
     values_local = jnp.dot(token_rows, wv, preferred_element_type=jnp.float32).astype(jnp.bfloat16)
     query_heads = queries.reshape(query_rows, heads_local, HD)
     running_max = jnp.full((heads_local, query_rows), -1e30, jnp.float32)
-    key_heads = lax.all_gather(keys_local, "band", axis=0, tiled=True).reshape(-1, heads_local, HD)
+    key_heads = jnp.concatenate(
+        lax.all_to_all(jnp.stack([keys_local] * lax.axis_size("band")), "band", 0, 0), axis=0
+    ).reshape(-1, heads_local, HD)
     value_heads = lax.all_gather(values_local, "band", axis=0, tiled=True).reshape(
         -1, heads_local, HD
     )

time: 734 us -> 713 us (0.971)
  waiting for transfers between devices: 523 us -> 468 us
  starting transfers between devices: 40.9 us -> 58.4 us
  local copies, waits for them, and re-layouts: 14.5 us -> 31.2 us
    all_to_all x0 -> x1, waiting for transfers between devices: none -> 105 us  [on_device(): lax.all_to_all(jnp.stack([keys_local] * lax.axis_size('band')), 'band', 0...]
    all_gather x1 -> x0, waiting for transfers between devices: 86.7 us -> none  [on_device(): lax.all_gather(keys_local, 'band', axis=0, tiled=True)]
    all_gather x1, waiting for transfers between devices: 68.6 us -> 0.02 us  [on_device(): lax.all_gather(values_local, 'band', axis=0, tiled=True)]
    all_to_all x0 -> x1, starting transfers between devices: none -> 14.3 us  [on_device(): lax.all_to_all(jnp.stack([keys_local] * lax.axis_size('band')), 'band', 0...]
    another operation x0 -> x2, local copies, waits for them, and re-layouts: none -> 9.93 us  [the longest x1 7.44 us: on_device(): key_heads = jnp.concatenate(lax.all_to_all(jnp.stack([keys_local] * lax.a...]
  transfers between devices with their start and end apart: 21 -> 21, of which waited for: 11 -> 10; matrix products, arithmetic and copies ran while one was open for 4% -> 7% of each run, Pallas kernels for 0% -> 0%
where the time goes in v1:
time: 713 us; the launch traced here: 711 us
  waiting for transfers between devices  468 us (66%)
  blocking collectives  84.1 us (12%)
  starting transfers between devices  58.4 us (8%)
  matrix products  35.3 us (5%)
  local copies, waits for them, and re-layouts  31.2 us (4%)
  other arithmetic  19.4 us (3%)
  between operations  14.4 us (2%)
    psum x1, waiting for transfers between devices, on_device(): lax.psum((first_terms, second_terms, bias_terms), ('band', 'var'))  250 us
    all_to_all x1, waiting for transfers between devices, on_device(): lax.all_to_all(jnp.stack([keys_local] * lax.axis_size('band')), 'band', 0...  105 us
    psum x1, waiting for transfers between devices, on_device(): lax.psum(partial_mix.astype(jnp.bfloat16), 'var').astype(jnp.float32)  85.5 us
    psum x1, blocking collectives, on_device(): lax.psum((first_terms, second_terms, bias_terms), ('band', 'var'))  84.1 us
    ppermute x8, starting transfers between devices, with_halo(): lax.ppermute(tail, axis, [(i, (i + 1) % count) for i in range(ends)])  30.8 us
    ppermute x8, waiting for transfers between devices, with_halo(): lax.ppermute(head, axis, [((i + 1) % count, i) for i in range(ends)])  15.2 us
    all_to_all x1, starting transfers between devices, on_device(): lax.all_to_all(jnp.stack([keys_local] * lax.axis_size('band')), 'band', 0...  14.3 us
  transfers between devices with their start and end apart: 21, of which 10 were waited for; matrix products, arithmetic and copies ran while one was open for 7% of the time, Pallas kernels for 0%

profile of v1, /device:TPU:1, one launch (start us, length us, event | category | flops | bytes accessed | tf_op | source)
XLA Modules:
  0.0 711.4 jit_solution(4450462033718046084)
XLA Ops:
  8.1 2.5 fusion.7
  10.6 85.5 %all-reduce.4.cloned.1.call-done = bf16[1,256,2048]{2,1,0:T(8,128)(2,1)} async-done(((bf16[1,256,2048]{2,1,0:T(8,128)(2,1)}), bf16[1,256,2048]{2,1,0:T(8,128)(2,1)}) %all-reduce.4.cloned.1.call-update) | async-done | bytes 1048592 | tf_op jit(solution)/shard_map/psum | solution.py:83
  99.8 2.5 stack.2
  102.3 14.3 %all-to-all-start = ((bf16[32,256,256]{1,2,0:T(8,128)(2,1)}), bf16[32,256,256]{1,2,0:T(8,128)(2,1)}, u32[]{:S(2)}, u32[]{:S(2)}) async-start(bf16[32,256,256]{1,2,0:T(8,128)(2,1)} %stack.2), calls=%async_computation | async-start | bytes 8388608 | tf_op jit(solution)/shard_map/all_to_all | solution.py:97
  119.6 104.7 %all-to-all-done = bf16[32,256,256]{1,2,0:T(8,128)(2,1)} async-done(((bf16[32,256,256]{1,2,0:T(8,128)(2,1)}), bf16[32,256,256]{1,2,0:T(8,128)(2,1)}, u32[]{:S(2)}, u32[]{:S(2)}) %all-to-all-start) | async-done | bytes 4194336 | tf_op jit(solution)/shard_map/all_to_all | solution.py:97
  224.3 6.6 copy.48
  230.9 7.4 %reshape_reshape.3 = bf16[8192,2,128]{0,2,1:T(8,128)(2,1)} reshape(bf16[32,256,256]{1,0,2:T(8,128)(2,1)} %copy.48) | data formatting | bytes 8388608 | tf_op jit(solution)/shard_map/reshape;reshape | solution.py:98
  238.3 10.4 %multiply_reduce_fusion = (f32[2,256]{1,0:T(2,128)S(1)}, f32[2,256,8192]{2,1,0:T(8,128)}) fusion(bf16[256,2,128]{0,2,1:T(8,128)(2,1)S(1)} %bitcast.111, bf16[8192,2,128]{0,2,1:T(8,128)(2,1)} %reshape_reshape.3), kind=kOutput, calls=%fused_computation.1 | convolution fusion | flops 1082129920 | bytes 21104640 | tf_op jit(solution)/shard_map/qhd,khd->hqk/dot_general | solution.py:102
  248.7 8.6 %fusion = f32[2,256]{1,0:T(2,128)S(1)} fusion(f32[2,256,8192]{2,1,0:T(8,128)} %get-tuple-element.32, f32[2,256]{1,0:T(2,128)S(1)} %broadcast_maximum_fusion), kind=kLoop, calls=%fused_computation.2 | loop fusion | flops 12582400 | bytes 16781312 | tf_op jit(solution)/shard_map/reduce_sum | solution.py:107
  257.3 6.4 copy.74
  263.7 10.4 %fusion.24 = bf16[256,2,128]{0,2,1:T(8,128)(2,1)S(1)} fusion(bf16[8192,2,128]{0,2,1:T(8,128)(2,1)} %bitcast.104, f32[2,256,8192]{2,1,0:T(8,128)} %get-tuple-element.32, f32[2,256]{1,0:T(2,128)S(1)} %broadcast_maximum_fusion, f32[256,2]{0,1:T(2,128)S(1)} %bitcast.119), kind=kOutput, calls=%fused_computation.35 | convolution fusion | flops 1086455808 | bytes 21106688 | tf_op jit(solution)/shard_map/hqk,khd->hqd/dot_general | solution.py:108
  275.7 6.6 collective-permute-start.8
  284.3 3.4 collective-permute-done.9
  300.5 11.0 %reduce-scatter.2.cloned.1.call-done = bf16[32,2048]{1,0:T(8,128)(2,1)} async-done(((bf16[256,2048]{1,0:T(8,128)(2,1)}), bf16[32,2048]{1,0:T(8,128)(2,1)}) %reduce-scatter.2.cloned.1.call-update) | async-done | bytes 131088 | tf_op jit(solution)/shard_map/reduce_scatter | solution.py:117
  311.5 3.1 convolution_convert_fusion.4
  314.9 8.6 %collective-permute-start = (bf16[1,64,128]{2,1,0:T(8,128)(2,1)S(1)}, bf16[1,64,128]{2,1,0:T(8,128)(2,1)S(1)}, u32[]{:S(2)}, u32[]{:S(2)}) collective-permute-start(bf16[1,64,128]{2,1,0:T(8,128)(2,1)S(1)} %copy.53), channel_id=1, source_target_pairs={{0,8},{8,16},{16,24},{24,32},{32,40},{40,48},{48,56},{56,64},{64,7... | collective-permute-start | bytes 49160 | tf_op jit(solution)/shard_map/ppermute | solution.py:21
  326.3 2.4 collective-permute-done.1
  332.3 3.1 collective-permute-done.3
  339.0 3.9 collective-permute-start.4
  344.9 3.6 collective-permute-start.12
  350.5 84.1 %psum.31 = f32[64]{0:T(128)} all-reduce(f32[64]{0:T(128)S(1)} %broadcast_multiply_fusion), channel_id=1, replica_groups=mesh['band'=32,'var'=8] {'band','var'}, use_global_device_ids=true, to_apply=%region_9.0 | all-reduce | flops 64 | bytes 512 | tf_op jit(solution)/shard_map/psum | solution.py:149
  437.8 4.0 collective-permute-start.14
  444.8 4.0 collective-permute-done.15
  451.3 250.1 %all-reduce.6.cloned.1.call-done = (f32[9,64,64]{2,1,0:T(8,128)}, f32[9,64,64]{2,1,0:T(8,128)}) async-done(((f32[9,64,64]{2,1,0:T(8,128)}, f32[9,64,64]{2,1,0:T(8,128)}), (f32[9,64,64]{2,1,0:T(8,128)}, f32[9,64,64]{2,1,0:T(8,128)})) %all-reduce.6.cloned.1.call-update) | async-done | bytes 294928 | tf_op jit(solution)/shard_map/psum | solution.py:149
  (131 shorter events, 49.7 us)
Async XLA Ops:
  7.2 267.0 %copy-start = (bf16[256,2048]{1,0:T(8,128)(2,1)S(1)}, bf16[256,2048]{1,0:T(8,128)(2,1)}, u32[]{:S(2)}) copy-start(bf16[256,2048]{1,0:T(8,128)(2,1)} %param.20) | copy-start | bytes 3145732
  7.2 92.1 %copy-start.2 = (bf16[2048,256]{1,0:T(8,128)(2,1)S(1)}, bf16[2048,256]{1,0:T(8,128)(2,1)}, u32[]{:S(2)}) copy-start(bf16[2048,256]{1,0:T(8,128)(2,1)} %param.18) | copy-start | bytes 3145732
  7.2 89.0 %all-reduce.4.cloned.1.call-start = ((), (), s32[]{:S(2)}) async-start(), calls=%async_computation.2 | async-start | bytes 2097152 | tf_op jit(solution)/shard_map/psum | solution.py:83
  102.3 122.0 %all-to-all-start = ((bf16[32,256,256]{1,2,0:T(8,128)(2,1)}), bf16[32,256,256]{1,2,0:T(8,128)(2,1)}, u32[]{:S(2)}, u32[]{:S(2)}) async-start(bf16[32,256,256]{1,2,0:T(8,128)(2,1)} %stack.2), calls=%async_computation | async-start | bytes 8388608 | tf_op jit(solution)/shard_map/all_to_all | solution.py:97
  116.6 140.7 %all-gather.2.cloned.1.call-start = ((), (), s32[]{:S(2)}) async-start(), calls=%async_computation.3 | async-start | bytes 4325376 | tf_op jit(solution)/shard_map/all_gather | solution.py:99
  117.8 193.7 %reduce-scatter.2.cloned.1.call-start = ((), (), s32[]{:S(2)}) async-start(), calls=%async_computation.4 | async-start | bytes 1179648 | tf_op jit(solution)/shard_map/reduce_scatter | solution.py:117
  275.6 425.8 %all-reduce.6.cloned.1.call-start = ((), (), s32[]{:S(2)}) async-start(), calls=%async_computation.5 | async-start | bytes 1179648 | tf_op jit(solution)/shard_map/psum | solution.py:149
  275.7 8.6 %collective-permute-start.8 = (bf16[1,64,128]{2,1,0:T(8,128)(2,1)S(1)}, bf16[1,64,128]{2,1,0:T(8,128)(2,1)S(1)}, u32[]{:S(2)}, u32[]{:S(2)}) collective-permute-start(bf16[1,64,128]{2,1,0:T(8,128)(2,1)S(1)} %get-tuple-element.28), channel_id=1, source_target_pairs={{0,8},{8,16},{16,24},{24,32},{32,40},{40,48},{48,56},{56,64},{64,7... | collective-permute-start | bytes 49160 | tf_op jit(solution)/shard_map/ppermute | solution.py:21
  282.3 5.5 collective-permute-start.9
  287.9 4.8 collective-permute-start.10
  289.5 7.5 %collective-permute-start.11 = (bf16[6,64,1]{2,1,0:T(8,128)(2,1)S(1)}, bf16[6,64,1]{2,1,0:T(8,128)(2,1)S(1)}, u32[]{:S(2)}, u32[]{:S(2)}) collective-permute-start(bf16[6,64,1]{2,1,0:T(8,128)(2,1)S(1)} %get-tuple-element.15), channel_id=1, source_target_pairs={{1,0},{2,1},{3,2},{4,3},{5,4},{6,5},{7,6},{9,8},{10,9},{11,10},{12... | collective-permute-start | bytes 2312 | tf_op jit(solution)/shard_map/ppermute | solution.py:23
  300.5 35.5 %copy-start.7 = (f32[64]{0:T(128)S(1)}, f32[64]{0:T(128)}, u32[]{:S(2)}) copy-start(f32[64]{0:T(128)} %param.23) | copy-start | bytes 772
  314.9 11.3 %collective-permute-start = (bf16[1,64,128]{2,1,0:T(8,128)(2,1)S(1)}, bf16[1,64,128]{2,1,0:T(8,128)(2,1)S(1)}, u32[]{:S(2)}, u32[]{:S(2)}) collective-permute-start(bf16[1,64,128]{2,1,0:T(8,128)(2,1)S(1)} %copy.53), channel_id=1, source_target_pairs={{0,8},{8,16},{16,24},{24,32},{32,40},{40,48},{48,56},{56,64},{64,7... | collective-permute-start | bytes 49160 | tf_op jit(solution)/shard_map/ppermute | solution.py:21
  323.6 5.1 collective-permute-start.1
  328.8 3.6 collective-permute-start.2
  330.1 5.4 collective-permute-start.3
  339.0 95.6 %collective-permute-start.4 = (bf16[1,64,128]{2,1,0:T(8,128)(2,1)S(1)}, bf16[1,64,128]{2,1,0:T(8,128)(2,1)S(1)}, u32[]{:S(2)}, u32[]{:S(2)}) collective-permute-start(bf16[1,64,128]{2,1,0:T(8,128)(2,1)S(1)} %get-tuple-element.29), channel_id=1, source_target_pairs={{0,8},{8,16},{16,24},{24,32},{32,40},{40,48},{48,56},{56,64},{64,7... | collective-permute-start | bytes 49160 | tf_op jit(solution)/shard_map/ppermute | solution.py:21
  343.0 91.7 %collective-permute-start.5 = (bf16[1,64,128]{2,1,0:T(8,128)(2,1)S(1)}, bf16[1,64,128]{2,1,0:T(8,128)(2,1)S(1)}, u32[]{:S(2)}, u32[]{:S(2)}) collective-permute-start(bf16[1,64,128]{2,1,0:T(8,128)(2,1)S(1)} %get-tuple-element.30), channel_id=1, source_target_pairs={{8,0},{16,8},{24,16},{32,24},{40,32},{48,40},{56,48},{64,56},{72,6... | collective-permute-start | bytes 49160 | tf_op jit(solution)/shard_map/ppermute | solution.py:23
  344.9 92.7 %collective-permute-start.12 = (bf16[1,64,128]{2,1,0:T(8,128)(2,1)S(1)}, bf16[1,64,128]{2,1,0:T(8,128)(2,1)S(1)}, u32[]{:S(2)}, u32[]{:S(2)}) collective-permute-start(bf16[1,64,128]{2,1,0:T(8,128)(2,1)S(1)} %get-tuple-element.25), channel_id=1, source_target_pairs={{0,8},{8,16},{16,24},{24,32},{32,40},{40,48},{48,56},{56,64},{64,7... | collective-permute-start | bytes 49160 | tf_op jit(solution)/shard_map/ppermute | solution.py:21
  348.5 89.1 %collective-permute-start.13 = (bf16[1,64,128]{2,1,0:T(8,128)(2,1)S(1)}, bf16[1,64,128]{2,1,0:T(8,128)(2,1)S(1)}, u32[]{:S(2)}, u32[]{:S(2)}) collective-permute-start(bf16[1,64,128]{2,1,0:T(8,128)(2,1)S(1)} %get-tuple-element.26), channel_id=1, source_target_pairs={{8,0},{16,8},{24,16},{32,24},{40,32},{48,40},{56,48},{64,56},{72,6... | collective-permute-start | bytes 49160 | tf_op jit(solution)/shard_map/ppermute | solution.py:23
  434.7 8.3 %collective-permute-start.6 = (bf16[6,64,1]{2,1,0:T(8,128)(2,1)S(1)}, bf16[6,64,1]{2,1,0:T(8,128)(2,1)S(1)}, u32[]{:S(2)}, u32[]{:S(2)}) collective-permute-start(bf16[6,64,1]{2,1,0:T(8,128)(2,1)S(1)} %get-tuple-element.20), channel_id=1, source_target_pairs={{0,1},{1,2},{2,3},{3,4},{4,5},{5,6},{6,7},{8,9},{9,10},{10,11},{11... | collective-permute-start | bytes 2312 | tf_op jit(solution)/shard_map/ppermute | solution.py:21
  436.3 6.8 collective-permute-start.7
  437.8 7.1 collective-permute-start.14
  441.8 7.1 %collective-permute-start.15 = (bf16[6,64,1]{2,1,0:T(8,128)(2,1)S(1)}, bf16[6,64,1]{2,1,0:T(8,128)(2,1)S(1)}, u32[]{:S(2)}, u32[]{:S(2)}) collective-permute-start(bf16[6,64,1]{2,1,0:T(8,128)(2,1)S(1)} %get-tuple-element.13), channel_id=1, source_target_pairs={{1,0},{2,1},{3,2},{4,3},{5,4},{6,5},{7,6},{9,8},{10,9},{11,10},{12... | collective-permute-start | bytes 2312 | tf_op jit(solution)/shard_map/ppermute | solution.py:23
  (5 other events, 70.9 us)
Sparse Core Ops, SparseCore 0:
  10.8 85.3 all-reduce.3
  120.8 109.8 all-gather.1
  275.7 35.7 reduce-scatter.1
  450.5 250.8 all-reduce.5
